TPU v7x, 32 devices: a whole 2x2x4 slice. The times are simulated.
32 devices in a mesh: shard: 8 (over z, x), tensor: 4 (over y, core).
Axes of the slice: x: 2, y: 2, z: 4, core: 2. Of those that a mesh axis runs over, the one named last changes fastest.
Arguments:
- matrix_grads: bfloat16 [56, 512, 2560], P(None, 'shard', 'tensor'), may hold values from -64 to 64
- matrix_momentum: float32 [56, 512, 2560], P(None, 'shard', 'tensor'), may hold values from -64 to 64
- matrix_weights: float32 [56, 512, 2560], P(None, 'shard', 'tensor'), may hold values from -6 to 6
- table_grads: bfloat16 [2048, 2560], P('shard', 'tensor'), may hold values from -6 to 6
- table_state: float32 [3, 2048, 2560], P(None, 'shard', 'tensor'), may hold values from -4 to 4, as said below
- small_grads: bfloat16 [120, 2560], P(None, 'tensor'), may hold values from -6 to 6
- small_state: float32 [3, 120, 2560], P(None, None, 'tensor'), may hold values from -4 to 4, as said below
Outputs:
- matrix_update: float32 [56, 512, 2560], P(None, 'shard', 'tensor')
- momentum_next: float32 [56, 512, 2560], P(None, 'shard', 'tensor')
- table_out: float32 [2, 2048, 2560], P(None, 'shard', 'tensor')
- small_out: float32 [2, 120, 2560], P(None, None, 'tensor')
Inputs may be any that keep to these rules, and one draw needn't show every extreme that they name: `table_state`: index 0 holds weights, index 1 first moments, index 2 second moments, which lie between 0.0002 and 0.004. `small_state`: index 0 holds weights, index 1 first moments, index 2 second moments, which lie between 0.0002 and 0.004.
All inputs are finite; a program needn't handle non-finite values.
Results may differ from a plain program's by a relative error of at most 0.014.
The roundings to bfloat16 on the way count: a program that leaves them out, or rounds other values in their place, can miss the bound.
Values may be sent and summed in bfloat16 or wider, within the bound.
A program may use at most 192 MiB of HBM per device.

v0:
```python
import math

import jax
import jax.numpy as jnp
from jax import lax
from jax.sharding import PartitionSpec as P

D = 2560
KV = 512
EXPERTS = 64
ITERS = 5


COEF_A = 3.4445
COEF_B = -4.775
COEF_C = 2.0315
BIAS_ONE = 1.0 - 0.9**10
BIAS_TWO = 1.0 - 0.999**10


def unchanged(values):
    return values


def newton_schulz(blended, square_total, gram_total):
    squares = square_total(jnp.sum(jnp.square(blended.astype(jnp.float32)), axis=(1, 2)))
    iterate = (blended.astype(jnp.float32) / (jnp.sqrt(squares) + 1e-07)[:, None, None]).astype(
        jnp.bfloat16
    )
    iterate = lax.optimization_barrier(iterate)
    for turn in range(ITERS):
        gram_term = jnp.einsum("krc,ksc->krs", iterate, iterate, preferred_element_type=jnp.float32)
        gram_matrix = gram_total(gram_term).astype(jnp.bfloat16)
        gram_matrix = lax.optimization_barrier(gram_matrix)
        gram_square = jnp.einsum(
            "krs,kst->krt", gram_matrix, gram_matrix, preferred_element_type=jnp.float32
        )
        polynomial = (COEF_B * gram_matrix.astype(jnp.float32) + COEF_C * gram_square).astype(
            jnp.bfloat16
        )
        product = jnp.einsum(
            "krs,ksc->krc", polynomial, iterate, preferred_element_type=jnp.float32
        )
        iterate = (COEF_A * iterate.astype(jnp.float32) + product).astype(jnp.bfloat16)
        iterate = lax.optimization_barrier(iterate)
    return iterate


def pad_matrices(blended, total):
    extra = total - blended.shape[0]
    filler = jnp.zeros((extra,) + blended.shape[1:], blended.dtype)
    return jnp.concatenate([blended, filler], axis=0)


def adamw(gradient, states, decay_rate):
    grad_value = gradient.astype(jnp.float32)
    moment_one = 0.9 * states[1] + 0.1 * grad_value
    moment_two = 0.999 * states[2] + 0.001 * grad_value * grad_value
    direction = (
        moment_one / BIAS_ONE / (jnp.sqrt(moment_two / BIAS_TWO) + 1e-08) + decay_rate * states[0]
    )
    return jnp.stack([direction, moment_one])


def local(
    matrix_grads,
    matrix_momentum,
    matrix_weights,
    table_grads,
    table_state,
    small_grads,
    small_state,
):
    momentum_next = 0.95 * matrix_momentum + matrix_grads.astype(jnp.float32)
    blended = (matrix_grads.astype(jnp.float32) + 0.95 * momentum_next).astype(jnp.bfloat16)
    matrix_count, rows_local, cols_local = blended.shape
    shards = lax.axis_size("shard")
    tensor_size = lax.axis_size("tensor")
    devices = shards * tensor_size
    per_device = -(-matrix_count // devices)
    padded = pad_matrices(blended, per_device * devices)
    source = padded.reshape(shards, tensor_size, per_device, rows_local, cols_local)
    arrived = lax.all_to_all(
        lax.all_to_all(source, "shard", split_axis=0, concat_axis=3, tiled=True),
        "tensor",
        split_axis=1,
        concat_axis=4,
        tiled=True,
    )
    whole_result = newton_schulz(arrived[0, 0], unchanged, unchanged)
    returned = lax.all_to_all(
        lax.all_to_all(whole_result[None, None], "shard", split_axis=3, concat_axis=0, tiled=True),
        "tensor",
        split_axis=4,
        concat_axis=1,
        tiled=True,
    )
    orthogonal = returned.reshape(devices * per_device, rows_local, cols_local)[:matrix_count]
    muon_scale = 0.2 * math.sqrt(max(KV, D))
    matrix_update = muon_scale * orthogonal.astype(jnp.float32) + 0.1 * matrix_weights
    table_out = adamw(table_grads, table_state, 0.1)
    row_index = jnp.arange(small_grads.shape[0], dtype=jnp.int32)
    small_decay = jnp.where(row_index < EXPERTS, 0.1, 0.0).astype(jnp.float32)[:, None]
    small_out = adamw(small_grads, small_state, small_decay)
    return (matrix_update, momentum_next, table_out, small_out)


def solution(mesh):
    placed = (
        P(None, "shard", "tensor"),
        P(None, "shard", "tensor"),
        P(None, "shard", "tensor"),
        P("shard", "tensor"),
        P(None, "shard", "tensor"),
        P(None, "tensor"),
        P(None, None, "tensor"),
    )
    return jax.shard_map(
        local,
        mesh=mesh,
        in_specs=placed,
        out_specs=(
            P(None, "shard", "tensor"),
            P(None, "shard", "tensor"),
            P(None, "shard", "tensor"),
            P(None, None, "tensor"),
        ),
        check_vma=False,
    )
```

profile of v0, /device:TPU:31, one launch (start us, length us, event | category | flops | bytes accessed | tf_op | source)
XLA Modules:
  0.0 589.6 jit_solution(7325919482131494463)
XLA Ops:
  0.6 12.7 %fusion.1 = (bf16[56,64,640]{2,1,0:T(8,128)(2,1)}, f32[56,64,640]{2,1,0:T(8,128)}) fusion(bf16[56,64,640]{2,1,0:T(8,128)(2,1)} %param.7, f32[56,64,640]{2,1,0:T(8,128)} %param.8), kind=kLoop, calls=%fused_computation.11 | loop fusion | flops 13762560 | bytes 27525120 | tf_op jit(solution)/shard_map/convert_element_type | solution.py:75
  13.3 3.0 concatenate.3
  16.3 118.7 %all_to_all.60 = bf16[8,4,2,64,640]{4,3,2,1,0:T(8,128)(2,1)S(1)} all-to-all(bf16[8,4,2,64,640]{4,3,2,1,0:T(8,128)(2,1)S(1)} %bitcast.89), channel_id=1, replica_groups=mesh['shard'=8,'tensor'=4] {'shard'}, dimensions={0} | all-to-all | bytes 10485760 | tf_op jit(solution)/shard_map/all_to_all | solution.py:84
  135.6 61.4 %all_to_all.61 = bf16[1,4,2,512,640]{4,3,2,0,1:T(8,128)(2,1)S(1)} all-to-all(bf16[1,4,2,512,640]{4,3,2,0,1:T(8,128)(2,1)S(1)} %bitcast.90), channel_id=1, replica_groups=mesh['shard'=8,'tensor'=4] {'tensor'}, dimensions={1} | all-to-all | bytes 10485760 | tf_op jit(solution)/shard_map/all_to_all | solution.py:83
  197.0 1.5 fusion
  198.5 4.5 convert_bitcast_fusion
  203.0 14.7 %copy.35 = f32[1,1,2,512,4,640]{5,4,3,2,1,0:T(4,128)} copy(f32[1,1,2,512,4,640]{5,3,2,4,1,0:T(8,128)} %convert_bitcast_fusion) | data formatting | bytes 20971520 | tf_op jit(solution)/shard_map/convert_element_type | solution.py:27
  217.7 13.0 %reshape.44 = f32[2,512,2560]{2,1,0:T(8,128)} reshape(f32[1,1,2,512,4,640]{5,4,3,2,1,0:T(4,128)} %copy.35) | data formatting | bytes 20971520 | tf_op jit(solution)/shard_map/convert_element_type | solution.py:27
  230.7 5.3 divide_convert_fusion
  236.0 2.3 copy-done
  238.4 2.9 convolution_convert_fusion.4
  241.3 8.5 %add_convert_fusion.4 = bf16[2,512,2560]{2,1,0:T(8,128)(2,1)} fusion(bf16[2,512,2560]{2,1,0:T(8,128)(2,1)} %copy-done, bf16[2,512,512]{2,1,0:T(8,128)(2,1)S(1)} %convolution_convert_fusion.4), kind=kOutput, calls=%fused_computation.9 | convolution fusion | flops 3234332672 | bytes 11534336 | tf_op jit(solution)/shard_map/krs,ksc->krc/dot_general | solution.py:41
  249.8 6.9 %convolution_convert_fusion.3 = bf16[2,512,512]{2,1,0:T(8,128)(2,1)S(1)} fusion(bf16[2,512,2560]{2,1,0:T(8,128)(2,1)} %add_convert_fusion.4), kind=kOutput, calls=%fused_computation.22 | convolution fusion | flops 2684878848 | bytes 6291456 | tf_op jit(solution)/shard_map/krc,ksc->krs/dot_general | solution.py:32
  256.7 8.4 %add_convert_fusion.3 = bf16[2,512,2560]{2,1,0:T(8,128)(2,1)} fusion(bf16[2,512,2560]{2,1,0:T(8,128)(2,1)} %add_convert_fusion.4, bf16[2,512,512]{2,1,0:T(8,128)(2,1)S(1)} %convolution_convert_fusion.3), kind=kOutput, calls=%fused_computation.8 | convolution fusion | flops 3234332672 | bytes 11534336 | tf_op jit(solution)/shard_map/krs,ksc->krc/dot_general | solution.py:41
  265.2 6.9 %convolution_convert_fusion.2 = bf16[2,512,512]{2,1,0:T(8,128)(2,1)S(1)} fusion(bf16[2,512,2560]{2,1,0:T(8,128)(2,1)} %add_convert_fusion.3), kind=kOutput, calls=%fused_computation.21 | convolution fusion | flops 2684878848 | bytes 6291456 | tf_op jit(solution)/shard_map/krc,ksc->krs/dot_general | solution.py:32
  272.1 8.9 %add_convert_fusion.2 = bf16[2,512,2560]{2,1,0:T(8,128)(2,1)} fusion(bf16[2,512,2560]{2,1,0:T(8,128)(2,1)} %add_convert_fusion.3, bf16[2,512,512]{2,1,0:T(8,128)(2,1)S(1)} %convolution_convert_fusion.2), kind=kOutput, calls=%fused_computation.7 | convolution fusion | flops 3234332672 | bytes 11534336 | tf_op jit(solution)/shard_map/krs,ksc->krc/dot_general | solution.py:41
  281.0 6.9 %convolution_convert_fusion.1 = bf16[2,512,512]{2,1,0:T(8,128)(2,1)S(1)} fusion(bf16[2,512,2560]{2,1,0:T(8,128)(2,1)} %add_convert_fusion.2), kind=kOutput, calls=%fused_computation.20 | convolution fusion | flops 2684878848 | bytes 6291456 | tf_op jit(solution)/shard_map/krc,ksc->krs/dot_general | solution.py:32
  287.9 8.4 %add_convert_fusion.1 = bf16[2,512,2560]{2,1,0:T(8,128)(2,1)} fusion(bf16[2,512,2560]{2,1,0:T(8,128)(2,1)} %add_convert_fusion.2, bf16[2,512,512]{2,1,0:T(8,128)(2,1)S(1)} %convolution_convert_fusion.1), kind=kOutput, calls=%fused_computation.6 | convolution fusion | flops 3234332672 | bytes 11534336 | tf_op jit(solution)/shard_map/krs,ksc->krc/dot_general | solution.py:41
  296.4 6.9 %convolution_convert_fusion = bf16[2,512,512]{2,1,0:T(8,128)(2,1)S(1)} fusion(bf16[2,512,2560]{2,1,0:T(8,128)(2,1)} %add_convert_fusion.1), kind=kOutput, calls=%fused_computation.19 | convolution fusion | flops 2684878848 | bytes 6291456 | tf_op jit(solution)/shard_map/krc,ksc->krs/dot_general | solution.py:32
  303.3 8.6 %add_convert_fusion = bf16[2,512,2560]{2,1,0:T(8,128)(2,1)} fusion(bf16[2,512,2560]{2,1,0:T(8,128)(2,1)} %add_convert_fusion.1, bf16[2,512,512]{2,1,0:T(8,128)(2,1)S(1)} %convolution_convert_fusion), kind=kOutput, calls=%fused_computation.5 | convolution fusion | flops 3234332672 | bytes 11534336 | tf_op jit(solution)/shard_map/krs,ksc->krc/dot_general | solution.py:41
  312.0 10.2 %copy.36 = bf16[1,1,2,512,2560]{4,2,1,0,3:T(2,128)(2,1)} copy(bf16[1,1,2,512,2560]{4,3,2,1,0:T(8,128)(2,1)} %bitcast.93) | data formatting | bytes 10485760 | tf_op jit(solution)/shard_map/broadcast_in_dim | solution.py:92
  322.2 120.1 %all_to_all.62 = bf16[1,1,2,512,2560]{4,2,1,0,3:T(2,128)(2,1)} all-to-all(bf16[1,1,2,512,2560]{4,2,1,0,3:T(2,128)(2,1)} %copy.36), channel_id=1, replica_groups=mesh['shard'=8,'tensor'=4] {'shard'}, dimensions={3} | all-to-all | bytes 10485760 | tf_op jit(solution)/shard_map/all_to_all | solution.py:92
  442.3 17.4 %copy.37 = bf16[1,1,2,8,64,2560]{4,3,2,5,1,0:T(8,128)(2,1)} copy(bf16[1,1,2,8,64,2560]{5,2,4,3,1,0:T(2,128)(2,1)} %bitcast.91) | data formatting | bytes 10485760 | tf_op jit(solution)/shard_map/all_to_all | solution.py:92
  459.8 10.4 %bitcast_bitcast_fusion = bf16[2560,1,2,8,64]{4,3,2,1,0:T(8,128)(2,1)} fusion(bf16[1,1,2,8,64,2560]{4,3,2,5,1,0:T(8,128)(2,1)} %copy.37), kind=kLoop, calls=%fused_computation.61 | loop fusion | bytes 10485760
  470.1 11.2 %reshape.46 = bf16[4,2,327680]{2,1,0:T(2,128)(2,1)} reshape(bf16[2560,1,2,8,64]{4,3,2,1,0:T(8,128)(2,1)} %bitcast_bitcast_fusion) | data formatting | bytes 10485760
  481.3 7.4 %all-to-all-start.3 = ((bf16[4,2,327680]{2,1,0:T(2,128)(2,1)}), bf16[4,2,327680]{2,1,0:T(2,128)(2,1)}, u32[]{:S(2)}, u32[]{:S(2)}) async-start(bf16[4,2,327680]{2,1,0:T(2,128)(2,1)} %reshape.46), calls=%async_computation.3 | async-start | bytes 10485760 | tf_op jit(solution)/shard_map/all_to_all | solution.py:91
  490.3 1.1 pad_maximum_fusion
  491.5 54.8 %all-to-all-done.3 = bf16[4,2,327680]{2,1,0:T(2,128)(2,1)} async-done(((bf16[4,2,327680]{2,1,0:T(2,128)(2,1)}), bf16[4,2,327680]{2,1,0:T(2,128)(2,1)}, u32[]{:S(2)}, u32[]{:S(2)}) %all-to-all-start.3) | async-done | bytes 5242912 | tf_op jit(solution)/shard_map/all_to_all | solution.py:91
  546.2 11.0 %reshape.47 = bf16[2560,1,2,8,64]{4,3,2,1,0:T(8,128)(2,1)} reshape(bf16[4,2,327680]{2,1,0:T(2,128)(2,1)} %all-to-all-done.3) | data formatting | bytes 10485760
  557.3 12.7 %copy.39 = bf16[8,1,2,64,4,640]{5,3,2,1,4,0:T(8,128)(2,1)} copy(bf16[8,1,2,64,4,640]{3,0,2,5,4,1:T(8,128)(2,1)} %bitcast.88) | data formatting | bytes 10485760 | tf_op jit(solution)/shard_map/all_to_all | solution.py:91
  570.0 7.1 %convert_multiply_fusion.1 = f32[7,4,1,2,64,640]{5,4,3,2,1,0:T(8,128)} fusion(bf16[8,4,1,2,64,640]{5,4,3,2,1,0:T(8,128)(2,1)} %bitcast.92), kind=kLoop, calls=%fused_computation.13 | loop fusion | flops 4587520 | bytes 13762560 | tf_op jit(solution)/shard_map/mul | solution.py:100
  577.0 12.4 %bitcast_add_fusion = f32[56,64,640]{2,1,0:T(8,128)} fusion(f32[7,4,1,2,64,640]{5,4,3,2,1,0:T(8,128)} %convert_multiply_fusion.1, f32[56,64,640]{2,1,0:T(8,128)} %param.9), kind=kLoop, calls=%fused_computation.12 | loop fusion | flops 4587520 | bytes 27525120 | tf_op jit(solution)/shard_map/add | solution.py:100
  (15 shorter events, 2.2 us)
Async XLA Ops:
  236.0 2.4 copy-start
  481.3 7.4 %copy-start.2 = (f32[3,120,640]{2,1,0:T(8,128)S(1)}, f32[3,120,640]{2,1,0:T(8,128)}, u32[]{:S(2)}) copy-start(f32[3,120,640]{2,1,0:T(8,128)} %param.13) | copy-start | bytes 2764804
  481.3 7.4 %copy-start.4 = (bf16[120,640]{1,0:T(8,128)(2,1)S(1)}, bf16[120,640]{1,0:T(8,128)(2,1)}, u32[]{:S(2)}) copy-start(bf16[120,640]{1,0:T(8,128)(2,1)} %param.12) | copy-start | bytes 460804
  481.3 8.5 %copy-start.1 = (f32[3,256,640]{2,1,0:T(8,128)S(1)}, f32[3,256,640]{2,1,0:T(8,128)}, u32[]{:S(2)}) copy-start(f32[3,256,640]{2,1,0:T(8,128)} %param.11) | copy-start | bytes 5898244
  481.3 8.5 %copy-start.3 = (bf16[256,640]{1,0:T(8,128)(2,1)S(1)}, bf16[256,640]{1,0:T(8,128)(2,1)}, u32[]{:S(2)}) copy-start(bf16[256,640]{1,0:T(8,128)(2,1)} %param.10) | copy-start | bytes 983044
  481.3 64.9 %all-to-all-start.3 = ((bf16[4,2,327680]{2,1,0:T(2,128)(2,1)}), bf16[4,2,327680]{2,1,0:T(2,128)(2,1)}, u32[]{:S(2)}, u32[]{:S(2)}) async-start(bf16[4,2,327680]{2,1,0:T(2,128)(2,1)} %reshape.46), calls=%async_computation.3 | async-start | bytes 10485760 | tf_op jit(solution)/shard_map/all_to_all | solution.py:91
where the time goes:
time: 599 us; the launch traced here: 590 us
  blocking collectives  300 us (50%)
  local copies, waits for them, and re-layouts  107 us (18%)
  matrix products  73.5 us (12%)
  waiting for transfers between devices  54.8 us (9%)
  other arithmetic  46.2 us (8%)
  starting transfers between devices  7.38 us (1%)
    all_to_all x1, blocking collectives, local(): lax.all_to_all(whole_result[None, None], 'shard', split_axis=3, concat_ax...  120 us
    all_to_all x1, blocking collectives, local(): lax.all_to_all(source, 'shard', split_axis=0, concat_axis=3, tiled=True)  119 us
    all_to_all x1, blocking collectives, local(): lax.all_to_all(lax.all_to_all(source, 'shard', split_axis=0, concat_axis=...  61.4 us
    all_to_all x1, waiting for transfers between devices, local(): lax.all_to_all(lax.all_to_all(whole_result[None, None], 'shard', split_ax...  54.8 us
    dot_general x5, matrix products, newton_schulz(): jnp.einsum('krs,ksc->krc', polynomial, iterate, preferred_element_type=jn...  42.8 us
    unnamed x13, local copies, waits for them, and re-layouts  34.9 us
    dot_general x5, matrix products, newton_schulz(): jnp.einsum('krc,ksc->krs', iterate, iterate, preferred_element_type=jnp.f...  30.7 us
    convert_element_type x2, local copies, waits for them, and re-layouts, newton_schulz(): blended.astype(jnp.float32) / (jnp.sqrt(squares) + 1e-07)[:, None, None]  27.7 us
  transfers between devices with their start and end apart: 1, of which 1 were waited for; matrix products, arithmetic and copies ran while one was open for 0% of the time, Pallas kernels for 0%

commit v1 on v0

v1 whole, which is shorter than its diff:
```python
import functools
import math

import jax
import jax.numpy as jnp
from jax import lax
from jax.experimental import pallas as pl
from jax.experimental.pallas import tpu as pltpu
from jax.sharding import PartitionSpec as P

D = 2560
KV = 512
EXPERTS = 64
ITERS = 5


COEF_A = 3.4445
COEF_B = -4.775
COEF_C = 2.0315
BIAS_ONE = 1.0 - 0.9**10
BIAS_TWO = 1.0 - 0.999**10

CHUNK = 512
MESH = pl.DeviceIdType.MESH


def orthogonalize(x, gram, root, poly):
    rows, cols = x.shape
    chunks = cols // CHUNK

    def columns(c):
        return pl.ds(pl.multiple_of(c * CHUNK, CHUNK), CHUNK)

    def add_squares(c, total):
        part = jnp.square(x[:, columns(c)].astype(jnp.float32))
        return total + jnp.sum(part, keepdims=True)

    squares = lax.fori_loop(0, chunks, add_squares, jnp.zeros((1, 1), jnp.float32))
    norm = jnp.sqrt(squares) + 1e-07

    def add_gram(part):
        gram[...] += lax.dot_general(
            part, part, (((1,), (1,)), ((), ())), preferred_element_type=jnp.float32
        )

    gram[...] = jnp.zeros_like(gram)

    def scale(c, carry):
        part = (x[:, columns(c)].astype(jnp.float32) / norm).astype(jnp.bfloat16)
        x[:, columns(c)] = part
        add_gram(part)
        return carry

    lax.fori_loop(0, chunks, scale, 0)

    def turn(t, carry):
        root[...] = gram[...].astype(jnp.bfloat16)
        square = jnp.dot(root[...], root[...], preferred_element_type=jnp.float32)
        poly[...] = (COEF_B * root[...].astype(jnp.float32) + COEF_C * square).astype(jnp.bfloat16)
        gram[...] = jnp.zeros_like(gram)

        def step(c, inner):
            part = x[:, columns(c)]
            product = jnp.dot(poly[...], part, preferred_element_type=jnp.float32)
            part = (COEF_A * part.astype(jnp.float32) + product).astype(jnp.bfloat16)
            x[:, columns(c)] = part

            @pl.when(t < ITERS - 1)
            def _():
                add_gram(part)

            return inner

        lax.fori_loop(0, chunks, step, 0)
        return carry

    lax.fori_loop(0, ITERS, turn, 0)


def muon_kernel(
    sizes,
    blended,
    result,
    whole,
    gram,
    root,
    poly,
    out_sem,
    in_sem,
    back_out_sem,
    back_in_sem,
):
    shards, tensor_size = sizes
    devices = shards * tensor_size
    count, rows, cols = blended.shape
    slots = whole.shape[0]
    shard = lax.axis_index("shard")
    tensor = lax.axis_index("tensor")
    me = shard * tensor_size + tensor
    last = slots - 1
    remainder = count - last * devices
    mine_last = (me * remainder + devices - 1) // devices
    has_last = (mine_last < remainder) & ((mine_last * devices) // remainder == me)

    def place(device):
        return (device // tensor_size, device % tensor_size)

    def block(slot, device):
        at_row, at_col = place(device)
        return whole.at[
            slot,
            pl.ds(pl.multiple_of(at_row * rows, rows), rows),
            pl.ds(pl.multiple_of(at_col * cols, cols), cols),
        ]

    barrier = pltpu.get_barrier_semaphore()

    def greet(i, carry):
        pl.semaphore_signal(
            barrier, inc=1, device_id=place((me + i) % devices), device_id_type=MESH
        )
        return carry

    lax.fori_loop(1, devices, greet, 0)
    pl.semaphore_wait(barrier, devices - 1)

    def outbound(slot, k, held):
        m = slot * devices + k
        home = (k * devices) // held
        return m, home, pltpu.make_async_remote_copy(
            src_ref=blended.at[m],
            dst_ref=block(slot, me),
            send_sem=out_sem.at[m],
            recv_sem=in_sem.at[slot],
            device_id=place(home),
            device_id_type=MESH,
        )

    for slot in range(slots):
        held = devices if slot < last else remainder
        first = (me * held) // devices

        def send(i, carry, slot=slot, held=held, first=first):
            k = (first + i) % held
            m, home, copy = outbound(slot, k, held)

            @pl.when(home != me)
            def _():
                copy.start()

            @pl.when(home == me)
            def _():
                pltpu.make_async_copy(blended.at[m], block(slot, me), in_sem.at[slot]).start()

            return carry

        lax.fori_loop(0, held, send, 0)

    def backward(slot, m, target):
        return pltpu.make_async_remote_copy(
            src_ref=block(slot, target),
            dst_ref=result.at[m],
            send_sem=back_out_sem.at[slot, target],
            recv_sem=back_in_sem.at[m],
            device_id=place(target),
            device_id_type=MESH,
        )

    def work(slot, carry):
        @pl.when((slot < last) | has_last)
        def _():
            m = slot * devices + jnp.where(slot < last, me, mine_last)
            whole_slot = whole.at[slot]
            pltpu.make_async_copy(whole_slot, whole_slot, in_sem.at[slot]).wait()
            orthogonalize(whole_slot, gram, root, poly)

            def send_back(i, inner):
                target = (me + i) % devices
                backward(slot, m, target).start()
                return inner

            lax.fori_loop(1, devices, send_back, 0)
            pltpu.make_async_copy(block(slot, me), result.at[m], back_in_sem.at[m]).start()

        return carry

    lax.fori_loop(0, slots, work, 0)

    for slot in range(slots):
        held = devices if slot < last else remainder

        def sent(k, carry, slot=slot, held=held):
            m, home, copy = outbound(slot, k, held)

            @pl.when(home != me)
            def _():
                copy.wait_send()

            return carry

        lax.fori_loop(0, held, sent, 0)

    def sent_back(slot, carry):
        @pl.when((slot < last) | has_last)
        def _():
            m = slot * devices + jnp.where(slot < last, me, mine_last)

            def one(i, inner):
                backward(slot, m, (me + i) % devices).wait_send()
                return inner

            lax.fori_loop(1, devices, one, 0)

        return carry

    lax.fori_loop(0, slots, sent_back, 0)

    def returned(m, carry):
        pltpu.make_async_copy(result.at[m], result.at[m], back_in_sem.at[m]).wait()
        return carry

    lax.fori_loop(0, count, returned, 0)


def muon(blended):
    shards = lax.axis_size("shard")
    tensor_size = lax.axis_size("tensor")
    devices = shards * tensor_size
    count, rows, cols = blended.shape
    slots = -(-count // devices)
    full_rows, full_cols = rows * shards, cols * tensor_size
    return pl.pallas_call(
        functools.partial(muon_kernel, (shards, tensor_size)),
        out_shape=jax.ShapeDtypeStruct(blended.shape, jnp.bfloat16),
        in_specs=[pl.BlockSpec(memory_space=pl.ANY)],
        out_specs=pl.BlockSpec(memory_space=pl.ANY),
        scratch_shapes=[
            pltpu.VMEM((slots, full_rows, full_cols), jnp.bfloat16),
            pltpu.VMEM((full_rows, full_rows), jnp.float32),
            pltpu.VMEM((full_rows, full_rows), jnp.bfloat16),
            pltpu.VMEM((full_rows, full_rows), jnp.bfloat16),
            pltpu.SemaphoreType.DMA((count,)),
            pltpu.SemaphoreType.DMA((slots,)),
            pltpu.SemaphoreType.DMA((slots, devices)),
            pltpu.SemaphoreType.DMA((count,)),
        ],
        compiler_params=pltpu.CompilerParams(
            collective_id=0, has_side_effects=True, vmem_limit_bytes=40 * 1024 * 1024
        ),
        name="muon",
    )(blended)


def adamw(gradient, states, decay_rate):
    grad_value = gradient.astype(jnp.float32)
    moment_one = 0.9 * states[1] + 0.1 * grad_value
    moment_two = 0.999 * states[2] + 0.001 * grad_value * grad_value
    direction = (
        moment_one / BIAS_ONE / (jnp.sqrt(moment_two / BIAS_TWO) + 1e-08) + decay_rate * states[0]
    )
    return jnp.stack([direction, moment_one])


def local(
    matrix_grads,
    matrix_momentum,
    matrix_weights,
    table_grads,
    table_state,
    small_grads,
    small_state,
):
    momentum_next = 0.95 * matrix_momentum + matrix_grads.astype(jnp.float32)
    blended = (matrix_grads.astype(jnp.float32) + 0.95 * momentum_next).astype(jnp.bfloat16)
    orthogonal = muon(blended)
    muon_scale = 0.2 * math.sqrt(max(KV, D))
    matrix_update = muon_scale * orthogonal.astype(jnp.float32) + 0.1 * matrix_weights
    table_out = adamw(table_grads, table_state, 0.1)
    row_index = jnp.arange(small_grads.shape[0], dtype=jnp.int32)
    small_decay = jnp.where(row_index < EXPERTS, 0.1, 0.0).astype(jnp.float32)[:, None]
    small_out = adamw(small_grads, small_state, small_decay)
    return (matrix_update, momentum_next, table_out, small_out)


def solution(mesh):
    placed = (
        P(None, "shard", "tensor"),
        P(None, "shard", "tensor"),
        P(None, "shard", "tensor"),
        P("shard", "tensor"),
        P(None, "shard", "tensor"),
        P(None, "tensor"),
        P(None, None, "tensor"),
    )
    return jax.shard_map(
        local,
        mesh=mesh,
        in_specs=placed,
        out_specs=(
            P(None, "shard", "tensor"),
            P(None, "shard", "tensor"),
            P(None, "shard", "tensor"),
            P(None, None, "tensor"),
        ),
        check_vma=False,
    )
```

time: 599 us -> 259 us (0.43); the launches traced: 590 us -> 259 us
  blocking collectives: 300 us -> 0 us
  Pallas kernels: 0 us -> 231 us
  local copies, waits for them, and re-layouts: 107 us -> 2.32 us
  matrix products: 73.5 us -> 0 us
  waiting for transfers between devices: 54.8 us -> 0 us
  other arithmetic: 46.2 us -> 25 us
  starting transfers between devices: 7.38 us -> 0 us
    all_to_all x3 -> x0, blocking collectives: 300 us -> none  [the longest x1 120 us: local(): lax.all_to_all(whole_result[None, None], 'shard', split_axis=3, concat_ax...]
    pallas_call x0 -> x1, Pallas kernels: none -> 231 us  [muon(): pl.pallas_call(functools.partial(muon_kernel, (shards, tensor_size)), out...]
    dot_general x10 -> x0, matrix products: 73.5 us -> none  [the longest x5 42.8 us: newton_schulz(): jnp.einsum('krs,ksc->krc', polynomial, iterate, preferred_element_type=jn...]
    all_to_all x1 -> x0, waiting for transfers between devices: 54.8 us -> none  [local(): lax.all_to_all(lax.all_to_all(whole_result[None, None], 'shard', split_ax...]
    unnamed x13 -> x10, local copies, waits for them, and re-layouts: 34.9 us -> 2.32 us
    all_to_all x3 -> x0, local copies, waits for them, and re-layouts: 30.7 us -> none  [the longest x1 17.4 us: local(): lax.all_to_all(whole_result[None, None], 'shard', split_axis=3, concat_ax...]
    convert_element_type x2 -> x0, local copies, waits for them, and re-layouts: 27.7 us -> none  [newton_schulz(): blended.astype(jnp.float32) / (jnp.sqrt(squares) + 1e-07)[:, None, None]]
    broadcast_in_dim x1 -> x0, local copies, waits for them, and re-layouts: 10.2 us -> none  [local(): whole_result[None, None]]
  transfers between devices with their start and end apart: 1 -> 0, of which waited for: 1 -> 0; matrix products, arithmetic and copies ran while one was open for 0% -> 0% of each run, Pallas kernels for 0% -> 0%
where the time goes in v1:
time: 259 us
  Pallas kernels  231 us (89%)
  other arithmetic  25 us (10%)
    pallas_call x1, Pallas kernels, muon(): pl.pallas_call(functools.partial(muon_kernel, (shards, tensor_size)), out...  231 us
    convert_element_type x1, other arithmetic, local(): (matrix_grads.astype(jnp.float32) + 0.95 * momentum_next).astype(jnp.bflo...  12.7 us
    add x1, other arithmetic, local(): muon_scale * orthogonal.astype(jnp.float32) + 0.1 * matrix_weights  9.58 us

profile of v1, /device:TPU:31, one launch (start us, length us, event | category | flops | bytes accessed | tf_op | source)
XLA Modules:
  0.0 259.3 jit_solution(911366202859035038)
XLA Ops:
  0.6 12.7 %fusion = (bf16[56,64,640]{2,1,0:T(8,128)(2,1)}, f32[56,64,640]{2,1,0:T(8,128)}) fusion(bf16[56,64,640]{2,1,0:T(8,128)(2,1)} %param.7, f32[56,64,640]{2,1,0:T(8,128)} %param.8), kind=kLoop, calls=%fused_computation.2 | loop fusion | flops 13762560 | bytes 27525120 | tf_op jit(solution)/shard_map/convert_element_type | solution.py:274
  13.3 0.0 copy-start
  13.3 2.3 copy-done
  15.6 231.3 %muon.1 = bf16[56,64,640]{2,1,0:T(8,128)(2,1)S(1)} custom-call(bf16[56,64,640]{2,1,0:T(8,128)(2,1)S(1)} %copy-done), custom_call_target="tpu_custom_call" | custom-call | tf_op jit(solution)/shard_map/muon/pallas_call | solution.py:232
  246.9 0.0 copy-start.1
  246.9 0.0 copy-start.3
  247.0 0.0 copy-start.2
  247.0 0.0 copy-start.4
  247.0 9.6 %multiply_add_fusion = f32[56,64,640]{2,1,0:T(8,128)} fusion(f32[56,64,640]{2,1,0:T(8,128)} %param.9, bf16[56,64,640]{2,1,0:T(8,128)(2,1)S(1)} %muon.1), kind=kLoop, calls=%fused_computation.3 | loop fusion | flops 9175040 | bytes 22937600 | tf_op jit(solution)/shard_map/add | solution.py:277
  256.6 0.0 copy-done.1
  256.6 0.0 copy-done.3
  256.6 0.5 fusion.8
  257.1 1.1 pad_maximum_fusion
  258.2 0.0 copy-done.2
  258.2 0.0 copy-done.4
  258.2 0.2 fusion.17
  258.4 0.9 pad_maximum_fusion.1
  (1 shorter events, 0.0 us)
Async XLA Ops:
  13.3 2.3 copy-start
  246.9 9.6 %copy-start.1 = (f32[3,256,640]{2,1,0:T(8,128)S(1)}, f32[3,256,640]{2,1,0:T(8,128)}, u32[]{:S(2)}) copy-start(f32[3,256,640]{2,1,0:T(8,128)} %param.11) | copy-start | bytes 5898244
  246.9 9.6 %copy-start.3 = (bf16[256,640]{1,0:T(8,128)(2,1)S(1)}, bf16[256,640]{1,0:T(8,128)(2,1)}, u32[]{:S(2)}) copy-start(bf16[256,640]{1,0:T(8,128)(2,1)} %param.10) | copy-start | bytes 983044
  247.0 11.2 %copy-start.2 = (f32[3,120,640]{2,1,0:T(8,128)S(1)}, f32[3,120,640]{2,1,0:T(8,128)}, u32[]{:S(2)}) copy-start(f32[3,120,640]{2,1,0:T(8,128)} %param.13) | copy-start | bytes 2764804
  247.0 11.2 %copy-start.4 = (bf16[120,640]{1,0:T(8,128)(2,1)S(1)}, bf16[120,640]{1,0:T(8,128)(2,1)}, u32[]{:S(2)}) copy-start(bf16[120,640]{1,0:T(8,128)(2,1)} %param.12) | copy-start | bytes 460804

commit v2 on v1

--- a/solution.py
+++ b/solution.py
@@ -77,14 +77,42 @@
     lax.fori_loop(0, ITERS, turn, 0)
 
 
+LANES = 8
+OUT_STRIDE = 5
+BACK_STRIDE = 13
+
+
+def rotation(step, first, held, stride):
+    while math.gcd(stride, held) > 1:
+        stride += 1
+    return (first + (step + 1) * stride) % held
+
+
+def inverse(step, first, held, stride):
+    while math.gcd(stride, held) > 1:
+        stride += 1
+    return (first + (held - 1 - step) * stride) % held
+
+
 def muon_kernel(
     sizes,
-    blended,
-    result,
+    grads,
+    momentum,
+    weights,
+    update,
+    momentum_next,
     whole,
     gram,
     root,
     poly,
+    blended,
+    result,
+    grad_lane,
+    read_lane,
+    write_lane,
+    grad_sem,
+    read_sem,
+    write_sem,
     out_sem,
     in_sem,
     back_out_sem,
@@ -92,7 +120,7 @@
 ):
     shards, tensor_size = sizes
     devices = shards * tensor_size
-    count, rows, cols = blended.shape
+    count, rows, cols = grads.shape
     slots = whole.shape[0]
     shard = lax.axis_index("shard")
     tensor = lax.axis_index("tensor")
@@ -101,6 +129,8 @@
     remainder = count - last * devices
     mine_last = (me * remainder + devices - 1) // devices
     has_last = (mine_last < remainder) & ((mine_last * devices) // remainder == me)
+    muon_scale = 0.2 * math.sqrt(max(whole.shape[1], whole.shape[2]))
+    lanes = grad_lane.shape[0]
 
     def place(device):
         return (device // tensor_size, device % tensor_size)
@@ -113,6 +143,42 @@
             pl.ds(pl.multiple_of(at_col * cols, cols), cols),
         ]
 
+    def item(i, back):
+        slot = i // devices
+        step = i % devices
+        first = (me * remainder) // devices
+        if back:
+            k_full = inverse(step, me, devices, BACK_STRIDE)
+            k_last = inverse(step % remainder, first, remainder, BACK_STRIDE)
+        else:
+            k_full = rotation(step, me, devices, OUT_STRIDE)
+            k_last = rotation(step, first, remainder, OUT_STRIDE)
+        k = jnp.where(slot < last, k_full, k_last)
+        home = jnp.where(slot < last, k_full, (k_last * devices) // remainder)
+        return slot, slot * devices + k, home
+
+    def read_grads(i):
+        m = item(i, False)[1]
+        lane = i % lanes
+        return pltpu.make_async_copy(grads.at[m], grad_lane.at[lane], grad_sem.at[lane])
+
+    def read_from(source, i, back):
+        m = item(i, back)[1]
+        lane = i % lanes
+        return pltpu.make_async_copy(source.at[m], read_lane.at[lane], read_sem.at[lane])
+
+    def write_to(target, i, back):
+        m = item(i, back)[1]
+        lane = i % lanes
+        return pltpu.make_async_copy(write_lane.at[lane], target.at[m], write_sem.at[lane])
+
+    def open_blend(i, carry):
+        read_grads(i).start()
+        read_from(momentum, i, False).start()
+        return carry
+
+    lax.fori_loop(0, lanes, open_blend, 0)
+
     barrier = pltpu.get_barrier_semaphore()
 
     def greet(i, carry):
@@ -124,10 +190,8 @@
     lax.fori_loop(1, devices, greet, 0)
     pl.semaphore_wait(barrier, devices - 1)
 
-    def outbound(slot, k, held):
-        m = slot * devices + k
-        home = (k * devices) // held
-        return m, home, pltpu.make_async_remote_copy(
+    def outbound(slot, m, home):
+        return pltpu.make_async_remote_copy(
             src_ref=blended.at[m],
             dst_ref=block(slot, me),
             send_sem=out_sem.at[m],
@@ -136,25 +200,50 @@
             device_id_type=MESH,
         )
 
-    for slot in range(slots):
-        held = devices if slot < last else remainder
-        first = (me * held) // devices
-
-        def send(i, carry, slot=slot, held=held, first=first):
-            k = (first + i) % held
-            m, home, copy = outbound(slot, k, held)
-
-            @pl.when(home != me)
-            def _():
-                copy.start()
-
-            @pl.when(home == me)
-            def _():
-                pltpu.make_async_copy(blended.at[m], block(slot, me), in_sem.at[slot]).start()
-
-            return carry
-
-        lax.fori_loop(0, held, send, 0)
+    def blend(i, carry):
+        slot, m, home = item(i, False)
+        lane = i % lanes
+        read_grads(i).wait()
+        read_from(momentum, i, False).wait()
+
+        @pl.when(i >= lanes)
+        def _():
+            write_to(momentum_next, i - lanes, False).wait()
+
+        grad = grad_lane[lane].astype(jnp.float32)
+        moment = 0.95 * read_lane[lane] + grad
+        write_lane[lane] = moment
+        blended[m] = (grad + 0.95 * moment).astype(jnp.bfloat16)
+        write_to(momentum_next, i, False).start()
+
+        @pl.when(home != me)
+        def _():
+            outbound(slot, m, home).start()
+
+        @pl.when(home == me)
+        def _():
+            pltpu.make_async_copy(blended.at[m], block(slot, me), in_sem.at[slot]).start()
+
+        @pl.when(i + lanes < count)
+        def _():
+            read_grads(i + lanes).start()
+            read_from(momentum, i + lanes, False).start()
+
+        return carry
+
+    lax.fori_loop(0, count, blend, 0)
+
+    def close_blend(i, carry):
+        write_to(momentum_next, i, False).wait()
+        return carry
+
+    lax.fori_loop(count - lanes, count, close_blend, 0)
+
+    def open_update(i, carry):
+        read_from(weights, i, True).start()
+        return carry
+
+    lax.fori_loop(0, lanes, open_update, 0)
 
     def backward(slot, m, target):
         return pltpu.make_async_remote_copy(
@@ -175,30 +264,52 @@
             orthogonalize(whole_slot, gram, root, poly)
 
             def send_back(i, inner):
-                target = (me + i) % devices
-                backward(slot, m, target).start()
+                target = rotation(i, me, devices, BACK_STRIDE)
+
+                @pl.when(target != me)
+                def _():
+                    backward(slot, m, target).start()
+
                 return inner
 
-            lax.fori_loop(1, devices, send_back, 0)
+            lax.fori_loop(0, devices, send_back, 0)
             pltpu.make_async_copy(block(slot, me), result.at[m], back_in_sem.at[m]).start()
 
         return carry
 
     lax.fori_loop(0, slots, work, 0)
 
-    for slot in range(slots):
-        held = devices if slot < last else remainder
-
-        def sent(k, carry, slot=slot, held=held):
-            m, home, copy = outbound(slot, k, held)
-
-            @pl.when(home != me)
-            def _():
-                copy.wait_send()
-
-            return carry
-
-        lax.fori_loop(0, held, sent, 0)
+    def finish(i, carry):
+        m = item(i, True)[1]
+        lane = i % lanes
+        read_from(weights, i, True).wait()
+        pltpu.make_async_copy(result.at[m], result.at[m], back_in_sem.at[m]).wait()
+
+        @pl.when(i >= lanes)
+        def _():
+            write_to(update, i - lanes, True).wait()
+
+        write_lane[lane] = muon_scale * result[m].astype(jnp.float32) + 0.1 * read_lane[lane]
+        write_to(update, i, True).start()
+
+        @pl.when(i + lanes < count)
+        def _():
+            read_from(weights, i + lanes, True).start()
+
+        return carry
+
+    lax.fori_loop(0, count, finish, 0)
+
+    def sent(i, carry):
+        slot, m, home = item(i, False)
+
+        @pl.when(home != me)
+        def _():
+            outbound(slot, m, home).wait_send()
+
+        return carry
+
+    lax.fori_loop(0, count, sent, 0)
 
     def sent_back(slot, carry):
         @pl.when((slot < last) | has_last)
@@ -215,40 +326,50 @@
 
     lax.fori_loop(0, slots, sent_back, 0)
 
-    def returned(m, carry):
-        pltpu.make_async_copy(result.at[m], result.at[m], back_in_sem.at[m]).wait()
-        return carry
-
-    lax.fori_loop(0, count, returned, 0)
-
-
-def muon(blended):
+    def close_update(i, carry):
+        write_to(update, i, True).wait()
+        return carry
+
+    lax.fori_loop(count - lanes, count, close_update, 0)
+
+
+def muon(grads, momentum, weights):
     shards = lax.axis_size("shard")
     tensor_size = lax.axis_size("tensor")
     devices = shards * tensor_size
-    count, rows, cols = blended.shape
+    count, rows, cols = grads.shape
     slots = -(-count // devices)
     full_rows, full_cols = rows * shards, cols * tensor_size
+    lanes = min(LANES, count)
+    anywhere = pl.BlockSpec(memory_space=pl.ANY)
     return pl.pallas_call(
         functools.partial(muon_kernel, (shards, tensor_size)),
-        out_shape=jax.ShapeDtypeStruct(blended.shape, jnp.bfloat16),
-        in_specs=[pl.BlockSpec(memory_space=pl.ANY)],
-        out_specs=pl.BlockSpec(memory_space=pl.ANY),
+        out_shape=[jax.ShapeDtypeStruct(grads.shape, jnp.float32)] * 2,
+        in_specs=[pl.BlockSpec(memory_space=pltpu.HBM)] * 3,
+        out_specs=[anywhere] * 2,
         scratch_shapes=[
             pltpu.VMEM((slots, full_rows, full_cols), jnp.bfloat16),
             pltpu.VMEM((full_rows, full_rows), jnp.float32),
             pltpu.VMEM((full_rows, full_rows), jnp.bfloat16),
             pltpu.VMEM((full_rows, full_rows), jnp.bfloat16),
+            pltpu.VMEM((count, rows, cols), jnp.bfloat16),
+            pltpu.VMEM((count, rows, cols), jnp.bfloat16),
+            pltpu.VMEM((lanes, rows, cols), jnp.bfloat16),
+            pltpu.VMEM((lanes, rows, cols), jnp.float32),
+            pltpu.VMEM((lanes, rows, cols), jnp.float32),
+            pltpu.SemaphoreType.DMA((lanes,)),
+            pltpu.SemaphoreType.DMA((lanes,)),
+            pltpu.SemaphoreType.DMA((lanes,)),
             pltpu.SemaphoreType.DMA((count,)),
             pltpu.SemaphoreType.DMA((slots,)),
             pltpu.SemaphoreType.DMA((slots, devices)),
             pltpu.SemaphoreType.DMA((count,)),
         ],
         compiler_params=pltpu.CompilerParams(
-            collective_id=0, has_side_effects=True, vmem_limit_bytes=40 * 1024 * 1024
+            collective_id=0, has_side_effects=True, vmem_limit_bytes=28 * 1024 * 1024
         ),
         name="muon",
-    )(blended)
+    )(grads, momentum, weights)
 
 
 def adamw(gradient, states, decay_rate):
@@ -270,11 +391,7 @@
     small_grads,
     small_state,
 ):
-    momentum_next = 0.95 * matrix_momentum + matrix_grads.astype(jnp.float32)
-    blended = (matrix_grads.astype(jnp.float32) + 0.95 * momentum_next).astype(jnp.bfloat16)
-    orthogonal = muon(blended)
-    muon_scale = 0.2 * math.sqrt(max(KV, D))
-    matrix_update = muon_scale * orthogonal.astype(jnp.float32) + 0.1 * matrix_weights
+    matrix_update, momentum_next = muon(matrix_grads, matrix_momentum, matrix_weights)
     table_out = adamw(table_grads, table_state, 0.1)
     row_index = jnp.arange(small_grads.shape[0], dtype=jnp.int32)
     small_decay = jnp.where(row_index < EXPERTS, 0.1, 0.0).astype(jnp.float32)[:, None]

time: 259 us -> 248 us (0.958); the launches traced: 259 us -> 245 us
  other arithmetic: 25 us -> 2.74 us
  local copies, waits for them, and re-layouts: 2.32 us -> 9.62 us
    convert_element_type x1 -> x0, other arithmetic: 12.7 us -> none  [local(): (matrix_grads.astype(jnp.float32) + 0.95 * momentum_next).astype(jnp.bflo...]
    add x1 -> x0, other arithmetic: 9.58 us -> none  [local(): muon_scale * orthogonal.astype(jnp.float32) + 0.1 * matrix_weights]
    unnamed x10 -> x12, local copies, waits for them, and re-layouts: 2.32 us -> 9.62 us
where the time goes in v2:
time: 248 us; the launch traced here: 245 us
  Pallas kernels  231 us (93%)
  local copies, waits for them, and re-layouts  9.62 us (4%)
  other arithmetic  2.74 us (1%)
    pallas_call x1, Pallas kernels, muon(): pl.pallas_call(functools.partial(muon_kernel, (shards, tensor_size)), out...  231 us
    unnamed x12, local copies, waits for them, and re-layouts  9.62 us

profile of v2, /device:TPU:31, one launch (start us, length us, event | category | flops | bytes accessed | tf_op | source)
XLA Modules:
  0.0 244.5 jit_solution(12011959032854441668)
XLA Ops:
  0.6 0.0 copy-start
  0.6 2.3 copy-done
  2.9 0.0 copy-start.1
  2.9 0.0 copy-start.3
  2.9 231.5 %muon.1 = (f32[56,64,640]{2,1,0:T(8,128)S(1)}, f32[56,64,640]{2,1,0:T(8,128)S(1)}) custom-call(bf16[56,64,640]{2,1,0:T(8,128)(2,1)S(1)} %copy-done, f32[56,64,640]{2,1,0:T(8,128)} %momentum.1, f32[56,64,640]{2,1,0:T(8,128)} %weights.1), custom_call_target="tpu_custom_call" | custom-call | tf_op jit(solution)/shard_map/muon/pallas_call | solution.py:345
  234.4 0.0 copy-start.2
  234.4 0.0 copy-start.4
  234.5 0.0 copy-done.1
  234.5 0.0 copy-done.3
  234.5 0.5 fusion.7
  235.0 1.1 pad_maximum_fusion
  236.1 0.0 copy-done.2
  236.1 0.0 copy-done.4
  236.1 0.2 fusion.16
  236.4 0.9 pad_maximum_fusion.1
  237.2 3.7 %copy.13 = f32[56,64,640]{2,1,0:T(8,128)} copy(f32[56,64,640]{2,1,0:T(8,128)S(1)} %get-tuple-element.16) | data formatting | bytes 18350080
  240.9 3.7 %copy.14 = f32[56,64,640]{2,1,0:T(8,128)} copy(f32[56,64,640]{2,1,0:T(8,128)S(1)} %get-tuple-element.17) | data formatting | bytes 18350080
  (1 shorter events, 0.0 us)
Async XLA Ops:
  0.6 2.3 copy-start
  2.9 231.5 %copy-start.1 = (f32[3,256,640]{2,1,0:T(8,128)S(1)}, f32[3,256,640]{2,1,0:T(8,128)}, u32[]{:S(2)}) copy-start(f32[3,256,640]{2,1,0:T(8,128)} %param.11) | copy-start | bytes 5898244
  2.9 231.5 %copy-start.3 = (bf16[256,640]{1,0:T(8,128)(2,1)S(1)}, bf16[256,640]{1,0:T(8,128)(2,1)}, u32[]{:S(2)}) copy-start(bf16[256,640]{1,0:T(8,128)(2,1)} %param.10) | copy-start | bytes 983044
  234.4 1.7 copy-start.2
  234.4 1.7 copy-start.4

commit v3 on v2

--- a/solution.py
+++ b/solution.py
@@ -92,6 +92,10 @@
     while math.gcd(stride, held) > 1:
         stride += 1
     return (first + (held - 1 - step) * stride) % held
+
+
+def tilt(shard, tensor_size):
+    return (shard // 2) % 2 * (tensor_size // 2)
 
 
 def muon_kernel(
@@ -127,8 +131,9 @@
     me = shard * tensor_size + tensor
     last = slots - 1
     remainder = count - last * devices
-    mine_last = (me * remainder + devices - 1) // devices
-    has_last = (mine_last < remainder) & ((mine_last * devices) // remainder == me)
+    turned = shard * tensor_size + (tensor + tensor_size - tilt(shard, tensor_size)) % tensor_size
+    mine_last = (turned * remainder + devices - 1) // devices
+    has_last = (mine_last < remainder) & ((mine_last * devices) // remainder == turned)
     muon_scale = 0.2 * math.sqrt(max(whole.shape[1], whole.shape[2]))
     lanes = grad_lane.shape[0]
 
@@ -154,7 +159,10 @@
             k_full = rotation(step, me, devices, OUT_STRIDE)
             k_last = rotation(step, first, remainder, OUT_STRIDE)
         k = jnp.where(slot < last, k_full, k_last)
-        home = jnp.where(slot < last, k_full, (k_last * devices) // remainder)
+        at = (k_last * devices) // remainder
+        row, col = at // tensor_size, at % tensor_size
+        spread = row * tensor_size + (col + tilt(row, tensor_size)) % tensor_size
+        home = jnp.where(slot < last, k_full, spread)
         return slot, slot * devices + k, home
 
     def read_grads(i):
@@ -200,8 +208,24 @@
             device_id_type=MESH,
         )
 
+    def send(i, carry):
+        slot, m, home = item(i, False)
+
+        @pl.when(home != me)
+        def _():
+            outbound(slot, m, home).start()
+
+        @pl.when(home == me)
+        def _():
+            pltpu.make_async_copy(blended.at[m], block(slot, me), in_sem.at[slot]).start()
+
+        return carry
+
+    def arrival(slot):
+        pltpu.make_async_copy(whole.at[slot], whole.at[slot], in_sem.at[slot]).wait()
+
     def blend(i, carry):
-        slot, m, home = item(i, False)
+        m = item(i, False)[1]
         lane = i % lanes
         read_grads(i).wait()
         read_from(momentum, i, False).wait()
@@ -216,13 +240,9 @@
         blended[m] = (grad + 0.95 * moment).astype(jnp.bfloat16)
         write_to(momentum_next, i, False).start()
 
-        @pl.when(home != me)
-        def _():
-            outbound(slot, m, home).start()
-
-        @pl.when(home == me)
-        def _():
-            pltpu.make_async_copy(blended.at[m], block(slot, me), in_sem.at[slot]).start()
+        @pl.when(i < devices)
+        def _():
+            send(i, 0)
 
         @pl.when(i + lanes < count)
         def _():
@@ -244,6 +264,10 @@
         return carry
 
     lax.fori_loop(0, lanes, open_update, 0)
+
+    for slot in range(1, slots):
+        arrival(slot - 1)
+        lax.fori_loop(slot * devices, min((slot + 1) * devices, count), send, 0)
 
     def backward(slot, m, target):
         return pltpu.make_async_remote_copy(
@@ -260,7 +284,11 @@
         def _():
             m = slot * devices + jnp.where(slot < last, me, mine_last)
             whole_slot = whole.at[slot]
-            pltpu.make_async_copy(whole_slot, whole_slot, in_sem.at[slot]).wait()
+
+            @pl.when(slot == last)
+            def _():
+                arrival(last)
+
             orthogonalize(whole_slot, gram, root, poly)
 
             def send_back(i, inner):

time: 248 us -> 233 us (0.940)
  the two profiles are of different devices: /device:TPU:31 before, /device:TPU:3 now
where the time goes in v3:
time: 233 us
  Pallas kernels  220 us (94%)
  local copies, waits for them, and re-layouts  9.62 us (4%)
  other arithmetic  2.74 us (1%)
    pallas_call x1, Pallas kernels, muon(): pl.pallas_call(functools.partial(muon_kernel, (shards, tensor_size)), out...  220 us
    unnamed x12, local copies, waits for them, and re-layouts  9.62 us

profile of v3, /device:TPU:3, one launch (start us, length us, event | category | flops | bytes accessed | tf_op | source)
XLA Modules:
  0.0 232.6 jit_solution(1936022100968015175)
XLA Ops:
  0.6 0.0 copy-start
  0.6 2.3 copy-done
  2.9 0.0 copy-start.1
  2.9 0.0 copy-start.3
  2.9 219.5 %muon.1 = (f32[56,64,640]{2,1,0:T(8,128)S(1)}, f32[56,64,640]{2,1,0:T(8,128)S(1)}) custom-call(bf16[56,64,640]{2,1,0:T(8,128)(2,1)S(1)} %copy-done, f32[56,64,640]{2,1,0:T(8,128)} %momentum.1, f32[56,64,640]{2,1,0:T(8,128)} %weights.1), custom_call_target="tpu_custom_call" | custom-call | tf_op jit(solution)/shard_map/muon/pallas_call | solution.py:373
  222.4 0.0 copy-start.2
  222.5 0.0 copy-start.4
  222.5 0.0 copy-done.1
  222.5 0.0 copy-done.3
  222.5 0.5 fusion.7
  223.0 1.1 pad_maximum_fusion
  224.1 0.0 copy-done.2
  224.1 0.0 copy-done.4
  224.1 0.2 fusion.16
  224.4 0.9 pad_maximum_fusion.1
  225.2 3.7 %copy.13 = f32[56,64,640]{2,1,0:T(8,128)} copy(f32[56,64,640]{2,1,0:T(8,128)S(1)} %get-tuple-element.16) | data formatting | bytes 18350080
  228.9 3.7 %copy.14 = f32[56,64,640]{2,1,0:T(8,128)} copy(f32[56,64,640]{2,1,0:T(8,128)S(1)} %get-tuple-element.17) | data formatting | bytes 18350080
  (1 shorter events, 0.0 us)
Async XLA Ops:
  0.6 2.3 copy-start
  2.9 219.5 %copy-start.1 = (f32[3,256,640]{2,1,0:T(8,128)S(1)}, f32[3,256,640]{2,1,0:T(8,128)}, u32[]{:S(2)}) copy-start(f32[3,256,640]{2,1,0:T(8,128)} %param.11) | copy-start | bytes 5898244
  2.9 219.5 %copy-start.3 = (bf16[256,640]{1,0:T(8,128)(2,1)S(1)}, bf16[256,640]{1,0:T(8,128)(2,1)}, u32[]{:S(2)}) copy-start(bf16[256,640]{1,0:T(8,128)(2,1)} %param.10) | copy-start | bytes 983044
  222.4 1.7 copy-start.2
  222.5 1.7 copy-start.4
